TPU v7x, 32 devices: a whole 2x2x4 slice. The times are simulated.
32 devices in a mesh: pair: 4 (over x, core), tile: 8 (over z, y).
Axes of the slice: x: 2, y: 2, z: 4, core: 2. Of those that a mesh axis runs over, the one named last changes fastest.
Arguments:
- interferograms: float32 [1024, 64, 128], P(('pair', 'tile')), may hold values from -6 to 6
- coherence: int32 [2, 64, 128], P(None, 'pair', 'tile'), may hold values 0 or 1
- epochs: int32 [1024, 2], replicated, may hold values from 0 to 399, as said below
- track: int32 [1024], replicated, may hold values from 0 to 1, as said below
Outputs:
- displacement: float32 [2, 400, 64, 128], P(None, None, 'pair', 'tile')
Inputs may be any that keep to these rules, and one draw needn't show every extreme that they name: Each row names an earlier and a later epoch, 1 to 12 epochs apart; row 0 starts at epoch 0 and row 1023 ends at epoch 400 - 1. `track`: exactly 576 entries are 0.
All inputs are finite; a program needn't handle non-finite values. No bound on the sum of `coherence` on one device may be relied on, other than what follows from the above.
Results may differ from a plain program's by a relative error of at most 0.0013.
Values may be sent and summed in bfloat16 or wider, within the bound.
A program may use at most 128 MiB of HBM per device.

v0:
```python
import math

import jax
import jax.numpy as jnp
from jax import lax
from jax.sharding import PartitionSpec as P

NEPOCH = 400
RADIUS = 4
ROUNDS = 4
CG_STEPS = 2


ALPHA_EXP = 0.5
HUBER_EDGE = 0.5
TIKHONOV = 1.0
EPSILON = 1e-06


def padded_2(array, sides, width):
    for axis, dim in sides:
        peers, length = (lax.axis_size(axis), array.shape[dim])
        up = [(i, (i + 1) % peers) for i in range(peers - 1)]
        down = [(j, i) for i, j in up]
        last = lax.slice_in_dim(array, length - width, length, axis=dim)
        first = lax.slice_in_dim(array, 0, width, axis=dim)
        before = lax.ppermute(last, axis, up)
        after = lax.ppermute(first, axis, down)
        array = jnp.concatenate([before, array, after], axis=dim)
    return array


def spectral_tables(patch_len):
    index_all = jnp.arange(patch_len * patch_len, dtype=jnp.int32)
    row_of = index_all // patch_len
    col_of = index_all % patch_len
    phase_int = (row_of[:, None] * row_of[None, :] + col_of[:, None] * col_of[None, :]) % patch_len
    turn_angle = phase_int.astype(jnp.float32) * (2.0 * math.pi / patch_len)
    return (jnp.cos(turn_angle), jnp.sin(turn_angle))


def box_mean(field_in):
    total_sum = jnp.zeros_like(field_in)
    for shift_row in (-1, 0, 1):
        for shift_col in (-1, 0, 1):
            total_sum = total_sum + jnp.roll(field_in, (shift_row, shift_col), axis=(-2, -1))
    return total_sum / 9.0


def goldstein_flat(flat_cells, cosine, sine_table, patch_len):
    highest = lax.Precision.HIGHEST
    count_rows = flat_cells.shape[0]
    cell_count = patch_len * patch_len
    real_part = jnp.dot(flat_cells, cosine, precision=highest, preferred_element_type=jnp.float32)
    imag_part = -jnp.dot(
        flat_cells, sine_table, precision=highest, preferred_element_type=jnp.float32
    )
    magnitude = jnp.sqrt(real_part * real_part + imag_part * imag_part + 1.0)
    weights = (
        box_mean(magnitude.reshape(count_rows, patch_len, patch_len)).reshape(
            count_rows, cell_count
        )
        ** ALPHA_EXP
    )
    restored = (
        jnp.dot(real_part * weights, cosine, precision=highest, preferred_element_type=jnp.float32)
        - jnp.dot(
            imag_part * weights, sine_table, precision=highest, preferred_element_type=jnp.float32
        )
    ) / cell_count
    return (restored / jnp.mean(weights, axis=1, keepdims=True)).astype(jnp.bfloat16)


def design_matrix(epochs, track):
    earlier_epoch = epochs[:, 0]
    later_epoch = epochs[:, 1]
    ascending = track == 0
    up_coef = jnp.where(ascending, 0.8, 0.75).astype(jnp.float32)
    east_coef = jnp.where(ascending, -0.6, 0.66).astype(jnp.float32)
    epoch_ids = jnp.arange(NEPOCH, dtype=jnp.int32)
    change = (later_epoch[:, None] == epoch_ids[None, :]).astype(jnp.float32) - (
        earlier_epoch[:, None] == epoch_ids[None, :]
    ).astype(jnp.float32)
    return jnp.concatenate([up_coef[:, None] * change, east_coef[:, None] * change], axis=1)


def apply_design(field_in, matrix):
    return jnp.dot(
        matrix, field_in, precision=lax.Precision.HIGHEST, preferred_element_type=jnp.float32
    )


def apply_transpose(pair_values, matrix):
    return lax.dot_general(
        matrix,
        pair_values,
        (((0,), (0,)), ((), ())),
        precision=lax.Precision.HIGHEST,
        preferred_element_type=jnp.float32,
    )


def gauss_taps():
    offsets = jnp.arange(-RADIUS, RADIUS + 1).astype(jnp.float32)
    raw_taps = jnp.exp(-offsets * offsets / 8.0)
    return raw_taps / jnp.sum(raw_taps)


def rows_pass(padded, rows_out):
    tap_values = gauss_taps()
    along_rows = tap_values[0] * padded[:, 0:rows_out, :]
    for tap_index in range(1, 2 * RADIUS + 1):
        along_rows = (
            along_rows + tap_values[tap_index] * padded[:, tap_index : tap_index + rows_out, :]
        )
    return along_rows


def cols_pass(padded, cols_out):
    tap_values = gauss_taps()
    result_sum = tap_values[0] * padded[:, :, 0:cols_out]
    for tap_index in range(1, 2 * RADIUS + 1):
        result_sum = (
            result_sum + tap_values[tap_index] * padded[:, :, tap_index : tap_index + cols_out]
        )
    return result_sum


def invert(observed, mask_cells, epochs, track, smoother):
    matrix = design_matrix(epochs, track)
    measured = observed.astype(jnp.float32)
    pair_mask = jnp.where((track == 0)[:, None], mask_cells[0][None, :], mask_cells[1][None, :])
    solution = jnp.zeros((2 * NEPOCH, measured.shape[1]), jnp.float32)
    for outer_no in range(ROUNDS):
        misfit = measured - apply_design(solution, matrix)
        weights = pair_mask * HUBER_EDGE / jnp.maximum(jnp.abs(misfit), HUBER_EDGE)

        def normal_apply(field_in):
            return (
                apply_transpose(weights * apply_design(field_in, matrix), matrix)
                + TIKHONOV * field_in
            )

        residual = apply_transpose(weights * measured, matrix) - normal_apply(solution)
        direction = residual
        norm_now = jnp.sum(residual * residual, axis=0)
        for inner_no in range(CG_STEPS):
            mapped = normal_apply(direction)
            step_len = norm_now / (jnp.sum(direction * mapped, axis=0) + EPSILON)
            solution = solution + step_len * direction
            residual = residual - step_len * mapped
            if inner_no + 1 < CG_STEPS:
                norm_next = jnp.sum(residual * residual, axis=0)
                direction = residual + norm_next / (norm_now + EPSILON) * direction
                norm_now = norm_next
        solution = smoother(solution)
    return solution


def per_device(interferograms, coherence, epochs, track):
    rows_split = lax.axis_size("pair")
    cols_split = lax.axis_size("tile")
    local_pairs, full_rows, full_cols = interferograms.shape
    patch_len = full_rows // rows_split
    cell_count = patch_len * patch_len
    tile_count = rows_split * cols_split
    cosine, sine_table = spectral_tables(patch_len)
    blocks = interferograms.reshape(local_pairs, rows_split, patch_len, cols_split, patch_len)
    blocks = blocks.transpose(0, 1, 3, 2, 4).reshape(local_pairs, tile_count, cell_count)
    cleaned = goldstein_flat(blocks.reshape(-1, cell_count), cosine, sine_table, patch_len)
    received = lax.all_to_all(
        cleaned.reshape(local_pairs, tile_count, cell_count),
        ("pair", "tile"),
        split_axis=1,
        concat_axis=0,
        tiled=True,
    )
    observed = received.reshape(-1, cell_count)
    mask_cells = coherence.reshape(2, cell_count).astype(jnp.float32)

    def smoother(field_in):
        grid_form = field_in.reshape(-1, patch_len, patch_len)
        row_padded = padded_2(grid_form, (("pair", 1),), RADIUS)
        along_rows = rows_pass(row_padded, patch_len)
        col_padded = padded_2(along_rows, (("tile", 2),), RADIUS)
        smoothed = cols_pass(col_padded, patch_len)
        return smoothed.reshape(field_in.shape[0], -1)

    solution = invert(observed, mask_cells, epochs, track, smoother)
    return solution.reshape(2, NEPOCH, patch_len, patch_len)


def solution(mesh):
    placed = (P(("pair", "tile"), None, None), P(None, "pair", "tile"), P(), P())
    return jax.shard_map(
        per_device,
        mesh=mesh,
        in_specs=placed,
        out_specs=P(None, None, "pair", "tile"),
        check_vma=False,
    )
```

profile of v0, /device:TPU:9, one launch (start us, length us, event | category | flops | bytes accessed | tf_op | source)
XLA Modules:
  0.0 357.5 jit_solution(7374510063623225879)
XLA Ops:
  3.6 9.0 %copy.15 = f32[32,4,8,16,16]{4,3,2,1,0:T(8,128)} copy(f32[32,4,8,16,16]{0,4,2,3,1:T(8,128)} %bitcast.120) | data formatting | bytes 2097152 | tf_op jit(solution)/shard_map/transpose | solution.py:169
  12.6 6.3 %reshape_reshape.6 = f32[1024,256]{1,0:T(8,128)S(1)} reshape(f32[32,4,8,16,16]{4,3,2,1,0:T(8,128)} %copy.15) | data formatting | bytes 2097152 | tf_op jit(solution)/shard_map/reshape;reshape | solution.py:170
  35.3 6.3 %all-to-all-start = ((bf16[32,32,256]{2,0,1:T(8,128)(2,1)}), bf16[32,32,256]{2,0,1:T(8,128)(2,1)S(1)}, u32[]{:S(2)}, u32[]{:S(2)}) async-start(bf16[32,32,256]{2,0,1:T(8,128)(2,1)} %copy.16), calls=%async_computation | async-start | bytes 1048576 | tf_op jit(solution)/shard_map/all_to_all | solution.py:171
  45.6 3.7 %fusion.212 = f32[1024,256]{0,1:T(8,128)S(1)} fusion(f32[1024,800]{1,0:T(8,128)S(1)} %pad_maximum_fusion), kind=kOutput, calls=%fused_computation.407 | convolution fusion | flops 2516582400 | bytes 4325376 | tf_op jit(solution)/shard_map/dot_general | solution.py:88
  49.3 7.6 %all-to-all-done = bf16[32,32,256]{2,0,1:T(8,128)(2,1)S(1)} async-done(((bf16[32,32,256]{2,0,1:T(8,128)(2,1)}), bf16[32,32,256]{2,0,1:T(8,128)(2,1)S(1)}, u32[]{:S(2)}, u32[]{:S(2)}) %all-to-all-start) | async-done | bytes 524320 | tf_op jit(solution)/shard_map/all_to_all | solution.py:171
  57.3 8.2 %fusion.31 = f32[800,256]{1,0:T(8,128)S(1)} fusion(f32[1024,800]{1,0:T(8,128)} %copy-done, f32[1024,256]{0,1:T(8,128)S(1)} %copy.17, f32[1024,256]{0,1:T(8,128)S(1)} %fusion.212, f32[256]{0:T(256)S(1)} %broadcast_in_dim.78, f32[256]{0:T(256)S(1)} %broadcast_in_dim.76, pred[1024]{0:T(1024)(128)(4,1)S(1)} %get-tuple-element.16), kind=kOutput, calls=%fused_computation.179 | convolution fusion | flops 2518417408 | bytes 6196224 | tf_op jit(solution)/shard_map/dot_general | solution.py:94
  65.5 6.3 %convolution_subtract_fusion.4 = f32[800,256]{1,0:T(8,128)S(1)} fusion(f32[800,256]{1,0:T(8,128)S(1)} %fusion.31, f32[1024,800]{1,0:T(8,128)S(1)} %copy-done.1, f32[1024,256]{0,1:T(8,128)S(1)} %fusion.212, f32[1024,256]{0,1:T(8,128)S(1)} %copy.17, f32[256]{0:T(256)S(1)} %broadcast_in_dim.78, f32[256]{0:T(256)S(1)} %broadcast_in_dim.76, ...), kind=kOutput, calls=%fused_computation.118 | convolution fusion | flops 2518622208 | bytes 7015424 | tf_op jit(solution)/shard_map/dot_general | solution.py:94
  71.9 3.9 %convolution_multiply_fusion.7 = f32[1024,256]{0,1:T(8,128)S(1)} fusion(f32[1024,800]{1,0:T(8,128)S(1)} %copy-done.1, f32[800,256]{1,0:T(8,128)S(1)} %convolution_subtract_fusion.4, f32[1024,256]{0,1:T(8,128)S(1)} %copy.17, f32[1024,256]{0,1:T(8,128)S(1)} %fusion.212, f32[256]{0:T(256)S(1)} %broadcast_in_dim.78, f32[256]{0:T(256)S(1)} %broadcast_in_dim.76, ...), kind=kOutput, calls=%fused_computation.96 | convolution fusion | flops 2518417408 | bytes 7244800 | tf_op jit(solution)/shard_map/dot_general | solution.py:88
  75.8 6.4 %multiply_reduce_fusion.10 = (f32[256]{0:T(256)S(1)}, f32[256]{0:T(256)S(1)}, f32[800,256]{1,0:T(8,128)S(1)}) fusion(f32[800,256]{1,0:T(8,128)S(1)} %convolution_subtract_fusion.4, f32[1024,800]{1,0:T(8,128)S(1)} %copy-done.1, f32[1024,256]{0,1:T(8,128)S(1)} %convolution_multiply_fusion.7), kind=kOutput, calls=%fused_computation.404 | convolution fusion | flops 2517605888 | bytes 5965824 | tf_op jit(solution)/shard_map/dot_general | solution.py:94
  82.4 4.0 %convolution_multiply_fusion.6 = f32[1024,256]{0,1:T(8,128)S(1)} fusion(f32[1024,800]{1,0:T(8,128)S(1)} %copy-done.1, f32[800,256]{1,0:T(8,128)S(1)} %convolution_subtract_fusion.4, f32[800,256]{1,0:T(8,128)S(1)} %get-tuple-element.66, f32[256]{0:T(256)S(1)} %add_divide_fusion.10, f32[256]{0:T(256)S(1)} %add_divide_fusion.11, f32[1024,256]{0,1:T(8,128)S(1)} %copy.17, ...), kind=kOutput, calls=%fused_computation.95 | convolution fusion | flops 2519236608 | bytes 8066048 | tf_op jit(solution)/shard_map/dot_general | solution.py:88
  86.4 6.1 %fusion.9 = f32[256]{0:T(256)S(1)} fusion(f32[1024,800]{1,0:T(8,128)S(1)} %copy-done.1, f32[1024,256]{0,1:T(8,128)S(1)} %convolution_multiply_fusion.6, f32[800,256]{1,0:T(8,128)S(1)} %convolution_subtract_fusion.4, f32[256]{0:T(256)S(1)} %add_divide_fusion.10, f32[800,256]{1,0:T(8,128)S(1)} %get-tuple-element.66, f32[256]{0:T(256)S(1)} %add_divide_fusion.11), kind=kOutput, calls=%fused_computation.144 | convolution fusion | flops 2518015744 | bytes 5966848 | tf_op jit(solution)/shard_map/dot_general | solution.py:94
  99.2 4.1 %collective-permute-done.1 = f32[800,4,16]{0,2,1:T(8,128)S(1)} collective-permute-done((f32[800,4,16]{0,2,1:T(8,128)S(1)}, f32[800,4,16]{0,2,1:T(8,128)S(1)}, u32[]{:S(2)}, u32[]{:S(2)}) %collective-permute-start.1) | collective-permute-done | bytes 204832 | tf_op jit(solution)/shard_map/ppermute | solution.py:28
  103.3 6.0 %fusion.99 = f32[800,16,16]{0,2,1:T(8,128)S(1)} fusion(f32[800,16,16]{0,2,1:T(8,128)S(1)} %bitcast.128, f32[800,4,16]{0,2,1:T(8,128)S(1)} %collective-permute-done.1, f32[800,4,16]{0,2,1:T(8,128)S(1)} %collective-permute-done, f32[]{:T(128)} %bitcast.28, f32[]{:T(128)} %bitcast.27, f32[]{:T(128)} %bitcast.26, f32[]{:T(128)} %bitcast.25, f32[]{:T(128)} %bitcast.24, ...), kind=kLoop, calls=%fused_computation.253 | loop fusion | flops 5120000 | bytes 2048036 | tf_op jit(solution)/shard_map/add | solution.py:114
  111.6 4.0 %collective-permute-start.3 = (f32[800,16,4]{0,2,1:T(4,128)S(1)}, f32[800,16,4]{0,2,1:T(4,128)S(1)}, u32[]{:S(2)}, u32[]{:S(2)}) collective-permute-start(f32[800,16,4]{0,2,1:T(4,128)S(1)} %get-tuple-element.46), channel_id=1, source_target_pairs={{1,0},{2,1},{3,2},{4,3},{5,4},{6,5},{7,6},{9,8},{10,9},{11,10},{12... | collective-permute-start | bytes 614408 | tf_op jit(solution)/shard_map/ppermute | solution.py:28
  121.0 6.9 %fusion.179 = f32[800,16,16]{0,2,1:T(8,128)S(1)} fusion(f32[800,16,16]{0,2,1:T(8,128)S(1)} %fusion.99, f32[800,16,4]{0,2,1:T(4,128)S(1)} %collective-permute-done.3, f32[800,16,4]{0,2,1:T(4,128)S(1)} %collective-permute-done.2, f32[]{:T(128)} %bitcast.28, f32[]{:T(128)} %bitcast.27, f32[]{:T(128)} %bitcast.26, f32[]{:T(128)} %bitcast.25, f32[]{:T(128)} %bitcast.24, ...), kind=kLoop, calls=%fused_computation.333 | loop fusion | flops 5120000 | bytes 2048036 | tf_op jit(solution)/shard_map/add | solution.py:124
  127.9 3.7 %fusion.267 = f32[1024,256]{0,1:T(8,128)S(1)} fusion(f32[1024,800]{1,0:T(8,128)S(1)} %copy-done.2, f32[800,256]{0,1:T(8,128)S(1)} %bitcast.121), kind=kOutput, calls=%fused_computation.483 | convolution fusion | flops 2516582400 | bytes 5144576 | tf_op jit(solution)/shard_map/dot_general | solution.py:88
  132.8 8.4 %convolution_add_fusion.8 = f32[800,256]{1,0:T(8,128)S(1)} fusion(f32[800,256]{1,0:T(8,128)} %copy.27, f32[1024,800]{1,0:T(8,128)} %copy-done, f32[1024,256]{0,1:T(8,128)S(1)} %fusion.267, f32[1024,256]{0,1:T(8,128)S(1)} %copy.17, f32[256]{0:T(256)S(1)} %broadcast_in_dim.78, f32[256]{0:T(256)S(1)} %broadcast_in_dim.76, ...), kind=kOutput, calls=%fused_computation.113 | convolution fusion | flops 2518622208 | bytes 7015424 | tf_op jit(solution)/shard_map/dot_general | solution.py:94
  141.2 6.6 %convolution_subtract_fusion.3 = f32[800,256]{1,0:T(8,128)S(1)} fusion(f32[800,256]{1,0:T(8,128)S(1)} %convolution_add_fusion.8, f32[1024,800]{1,0:T(8,128)S(1)} %copy-done.3, f32[1024,256]{0,1:T(8,128)S(1)} %copy.17, f32[1024,256]{0,1:T(8,128)S(1)} %fusion.267, f32[256]{0:T(256)S(1)} %broadcast_in_dim.78, f32[256]{0:T(256)S(1)} %broadcast_in_dim.76, ...), kind=kOutput, calls=%fused_computation.114 | convolution fusion | flops 2518622208 | bytes 7015424 | tf_op jit(solution)/shard_map/dot_general | solution.py:94
  147.8 3.9 %convolution_multiply_fusion.5 = f32[1024,256]{0,1:T(8,128)S(1)} fusion(f32[1024,800]{1,0:T(8,128)S(1)} %copy-done.3, f32[800,256]{1,0:T(8,128)S(1)} %convolution_subtract_fusion.3, f32[1024,256]{0,1:T(8,128)S(1)} %copy.17, f32[1024,256]{0,1:T(8,128)S(1)} %fusion.267, f32[256]{0:T(256)S(1)} %broadcast_in_dim.78, f32[256]{0:T(256)S(1)} %broadcast_in_dim.76, ...), kind=kOutput, calls=%fused_computation.94 | convolution fusion | flops 2518417408 | bytes 7244800 | tf_op jit(solution)/shard_map/dot_general | solution.py:88
  151.7 6.2 %multiply_reduce_fusion.7 = (f32[256]{0:T(256)S(1)}, f32[256]{0:T(256)S(1)}, f32[800,256]{1,0:T(8,128)S(1)}) fusion(f32[800,256]{1,0:T(8,128)S(1)} %convolution_subtract_fusion.3, f32[1024,800]{1,0:T(8,128)S(1)} %copy-done.3, f32[1024,256]{0,1:T(8,128)S(1)} %convolution_multiply_fusion.5), kind=kOutput, calls=%fused_computation.398 | convolution fusion | flops 2517605888 | bytes 5965824 | tf_op jit(solution)/shard_map/dot_general | solution.py:94
  158.1 4.0 %convolution_multiply_fusion.4 = f32[1024,256]{0,1:T(8,128)S(1)} fusion(f32[1024,800]{1,0:T(8,128)S(1)} %copy-done.3, f32[800,256]{1,0:T(8,128)S(1)} %convolution_subtract_fusion.3, f32[800,256]{1,0:T(8,128)S(1)} %get-tuple-element.67, f32[256]{0:T(256)S(1)} %add_divide_fusion.7, f32[256]{0:T(256)S(1)} %add_divide_fusion.8, f32[1024,256]{0,1:T(8,128)S(1)} %copy.17, ...), kind=kOutput, calls=%fused_computation.93 | convolution fusion | flops 2519236608 | bytes 8066048 | tf_op jit(solution)/shard_map/dot_general | solution.py:88
  162.1 6.0 %fusion.10 = f32[256]{0:T(256)S(1)} fusion(f32[1024,800]{1,0:T(8,128)S(1)} %copy-done.3, f32[1024,256]{0,1:T(8,128)S(1)} %convolution_multiply_fusion.4, f32[800,256]{1,0:T(8,128)S(1)} %convolution_subtract_fusion.3, f32[256]{0:T(256)S(1)} %add_divide_fusion.7, f32[800,256]{1,0:T(8,128)S(1)} %get-tuple-element.67, f32[256]{0:T(256)S(1)} %add_divide_fusion.8), kind=kOutput, calls=%fused_computation.145 | convolution fusion | flops 2518015744 | bytes 5966848 | tf_op jit(solution)/shard_map/dot_general | solution.py:94
  174.4 4.4 %collective-permute-done.5 = f32[800,4,16]{0,2,1:T(8,128)S(1)} collective-permute-done((f32[800,4,16]{0,2,1:T(8,128)S(1)}, f32[800,4,16]{0,2,1:T(8,128)S(1)}, u32[]{:S(2)}, u32[]{:S(2)}) %collective-permute-start.5) | collective-permute-done | bytes 204832 | tf_op jit(solution)/shard_map/ppermute | solution.py:28
  178.8 6.0 %fusion.79 = f32[800,16,16]{0,2,1:T(8,128)S(1)} fusion(f32[800,16,16]{0,2,1:T(8,128)S(1)} %bitcast.130, f32[800,4,16]{0,2,1:T(8,128)S(1)} %collective-permute-done.5, f32[800,4,16]{0,2,1:T(8,128)S(1)} %collective-permute-done.4, f32[]{:T(128)} %bitcast.28, f32[]{:T(128)} %bitcast.27, f32[]{:T(128)} %bitcast.26, f32[]{:T(128)} %bitcast.25, f32[]{:T(128)} %bitcast.24, ...), kind=kLoop, calls=%fused_computation.233 | loop fusion | flops 5120000 | bytes 2048036 | tf_op jit(solution)/shard_map/add | solution.py:114
  186.9 4.3 %collective-permute-start.7 = (f32[800,16,4]{0,2,1:T(4,128)S(1)}, f32[800,16,4]{0,2,1:T(4,128)S(1)}, u32[]{:S(2)}, u32[]{:S(2)}) collective-permute-start(f32[800,16,4]{0,2,1:T(4,128)S(1)} %get-tuple-element.42), channel_id=1, source_target_pairs={{1,0},{2,1},{3,2},{4,3},{5,4},{6,5},{7,6},{9,8},{10,9},{11,10},{12... | collective-permute-start | bytes 614408 | tf_op jit(solution)/shard_map/ppermute | solution.py:28
  196.9 6.9 %fusion.159 = f32[800,16,16]{0,2,1:T(8,128)S(1)} fusion(f32[800,16,16]{0,2,1:T(8,128)S(1)} %fusion.79, f32[800,16,4]{0,2,1:T(4,128)S(1)} %collective-permute-done.7, f32[800,16,4]{0,2,1:T(4,128)S(1)} %collective-permute-done.6, f32[]{:T(128)} %bitcast.28, f32[]{:T(128)} %bitcast.27, f32[]{:T(128)} %bitcast.26, f32[]{:T(128)} %bitcast.25, f32[]{:T(128)} %bitcast.24, ...), kind=kLoop, calls=%fused_computation.313 | loop fusion | flops 5120000 | bytes 2048036 | tf_op jit(solution)/shard_map/add | solution.py:124
  203.8 3.7 %fusion.268 = f32[1024,256]{0,1:T(8,128)S(1)} fusion(f32[1024,800]{1,0:T(8,128)S(1)} %copy-done.4, f32[800,256]{0,1:T(8,128)S(1)} %bitcast.123), kind=kOutput, calls=%fused_computation.484 | convolution fusion | flops 2516582400 | bytes 5144576 | tf_op jit(solution)/shard_map/dot_general | solution.py:88
  208.7 8.4 %convolution_add_fusion.5 = f32[800,256]{1,0:T(8,128)S(1)} fusion(f32[800,256]{1,0:T(8,128)} %copy.34, f32[1024,800]{1,0:T(8,128)} %copy-done, f32[1024,256]{0,1:T(8,128)S(1)} %fusion.268, f32[1024,256]{0,1:T(8,128)S(1)} %copy.17, f32[256]{0:T(256)S(1)} %broadcast_in_dim.78, f32[256]{0:T(256)S(1)} %broadcast_in_dim.76, ...), kind=kOutput, calls=%fused_computation.108 | convolution fusion | flops 2518622208 | bytes 7015424 | tf_op jit(solution)/shard_map/dot_general | solution.py:94
  217.1 6.3 %convolution_subtract_fusion.2 = f32[800,256]{1,0:T(8,128)S(1)} fusion(f32[800,256]{1,0:T(8,128)S(1)} %convolution_add_fusion.5, f32[1024,800]{1,0:T(8,128)S(1)} %copy-done.5, f32[1024,256]{0,1:T(8,128)S(1)} %copy.17, f32[1024,256]{0,1:T(8,128)S(1)} %fusion.268, f32[256]{0:T(256)S(1)} %broadcast_in_dim.78, f32[256]{0:T(256)S(1)} %broadcast_in_dim.76, ...), kind=kOutput, calls=%fused_computation.109 | convolution fusion | flops 2518622208 | bytes 7015424 | tf_op jit(solution)/shard_map/dot_general | solution.py:94
  223.4 3.9 %convolution_multiply_fusion.3 = f32[1024,256]{0,1:T(8,128)S(1)} fusion(f32[1024,800]{1,0:T(8,128)S(1)} %copy-done.5, f32[800,256]{1,0:T(8,128)S(1)} %convolution_subtract_fusion.2, f32[1024,256]{0,1:T(8,128)S(1)} %copy.17, f32[1024,256]{0,1:T(8,128)S(1)} %fusion.268, f32[256]{0:T(256)S(1)} %broadcast_in_dim.78, f32[256]{0:T(256)S(1)} %broadcast_in_dim.76, ...), kind=kOutput, calls=%fused_computation.92 | convolution fusion | flops 2518417408 | bytes 7244800 | tf_op jit(solution)/shard_map/dot_general | solution.py:88
  227.4 6.4 %multiply_reduce_fusion.4 = (f32[256]{0:T(256)S(1)}, f32[256]{0:T(256)S(1)}, f32[800,256]{1,0:T(8,128)S(1)}) fusion(f32[800,256]{1,0:T(8,128)S(1)} %convolution_subtract_fusion.2, f32[1024,800]{1,0:T(8,128)S(1)} %copy-done.5, f32[1024,256]{0,1:T(8,128)S(1)} %convolution_multiply_fusion.3), kind=kOutput, calls=%fused_computation.392 | convolution fusion | flops 2517605888 | bytes 5965824 | tf_op jit(solution)/shard_map/dot_general | solution.py:94
  234.0 4.0 %convolution_multiply_fusion.2 = f32[1024,256]{0,1:T(8,128)S(1)} fusion(f32[1024,800]{1,0:T(8,128)S(1)} %copy-done.5, f32[800,256]{1,0:T(8,128)S(1)} %convolution_subtract_fusion.2, f32[800,256]{1,0:T(8,128)S(1)} %get-tuple-element.68, f32[256]{0:T(256)S(1)} %add_divide_fusion.4, f32[256]{0:T(256)S(1)} %add_divide_fusion.5, f32[1024,256]{0,1:T(8,128)S(1)} %copy.17, ...), kind=kOutput, calls=%fused_computation.91 | convolution fusion | flops 2519236608 | bytes 8066048 | tf_op jit(solution)/shard_map/dot_general | solution.py:88
  238.0 6.0 %fusion.11 = f32[256]{0:T(256)S(1)} fusion(f32[1024,800]{1,0:T(8,128)S(1)} %copy-done.5, f32[1024,256]{0,1:T(8,128)S(1)} %convolution_multiply_fusion.2, f32[800,256]{1,0:T(8,128)S(1)} %convolution_subtract_fusion.2, f32[256]{0:T(256)S(1)} %add_divide_fusion.4, f32[800,256]{1,0:T(8,128)S(1)} %get-tuple-element.68, f32[256]{0:T(256)S(1)} %add_divide_fusion.5), kind=kOutput, calls=%fused_computation.146 | convolution fusion | flops 2518015744 | bytes 5966848 | tf_op jit(solution)/shard_map/dot_general | solution.py:94
  250.0 4.4 %collective-permute-done.9 = f32[800,4,16]{0,2,1:T(8,128)S(1)} collective-permute-done((f32[800,4,16]{0,2,1:T(8,128)S(1)}, f32[800,4,16]{0,2,1:T(8,128)S(1)}, u32[]{:S(2)}, u32[]{:S(2)}) %collective-permute-start.9) | collective-permute-done | bytes 204832 | tf_op jit(solution)/shard_map/ppermute | solution.py:28
  254.4 6.0 %fusion.59 = f32[800,16,16]{0,2,1:T(8,128)S(1)} fusion(f32[800,16,16]{0,2,1:T(8,128)S(1)} %bitcast.132, f32[800,4,16]{0,2,1:T(8,128)S(1)} %collective-permute-done.9, f32[800,4,16]{0,2,1:T(8,128)S(1)} %collective-permute-done.8, f32[]{:T(128)} %bitcast.28, f32[]{:T(128)} %bitcast.27, f32[]{:T(128)} %bitcast.26, f32[]{:T(128)} %bitcast.25, f32[]{:T(128)} %bitcast.24, ...), kind=kLoop, calls=%fused_computation.213 | loop fusion | flops 5120000 | bytes 2048036 | tf_op jit(solution)/shard_map/add | solution.py:114
  262.6 4.1 %collective-permute-start.11 = (f32[800,16,4]{0,2,1:T(4,128)S(1)}, f32[800,16,4]{0,2,1:T(4,128)S(1)}, u32[]{:S(2)}, u32[]{:S(2)}) collective-permute-start(f32[800,16,4]{0,2,1:T(4,128)S(1)} %get-tuple-element.38), channel_id=1, source_target_pairs={{1,0},{2,1},{3,2},{4,3},{5,4},{6,5},{7,6},{9,8},{10,9},{11,10},{12... | collective-permute-start | bytes 614408 | tf_op jit(solution)/shard_map/ppermute | solution.py:28
  272.6 6.9 %fusion.139 = f32[800,16,16]{0,2,1:T(8,128)S(1)} fusion(f32[800,16,16]{0,2,1:T(8,128)S(1)} %fusion.59, f32[800,16,4]{0,2,1:T(4,128)S(1)} %collective-permute-done.11, f32[800,16,4]{0,2,1:T(4,128)S(1)} %collective-permute-done.10, f32[]{:T(128)} %bitcast.28, f32[]{:T(128)} %bitcast.27, f32[]{:T(128)} %bitcast.26, f32[]{:T(128)} %bitcast.25, f32[]{:T(128)} %bitcast.24, ...), kind=kLoop, calls=%fused_computation.293 | loop fusion | flops 5120000 | bytes 2048036 | tf_op jit(solution)/shard_map/add | solution.py:124
  284.4 8.4 %convolution_add_fusion.2 = f32[800,256]{1,0:T(8,128)S(1)} fusion(f32[800,256]{1,0:T(8,128)} %copy.41, f32[1024,800]{1,0:T(8,128)} %copy-done, f32[1024,256]{0,1:T(8,128)S(1)} %fusion.269, f32[1024,256]{0,1:T(8,128)S(1)} %copy.17, f32[256]{0:T(256)S(1)} %broadcast_in_dim.78, f32[256]{0:T(256)S(1)} %broadcast_in_dim.76, ...), kind=kOutput, calls=%fused_computation.103 | convolution fusion | flops 2518622208 | bytes 7015424 | tf_op jit(solution)/shard_map/dot_general | solution.py:94
  292.8 6.6 %convolution_subtract_fusion.1 = f32[800,256]{1,0:T(8,128)S(1)} fusion(f32[800,256]{1,0:T(8,128)S(1)} %convolution_add_fusion.2, f32[1024,800]{1,0:T(8,128)S(1)} %copy-done.7, f32[1024,256]{0,1:T(8,128)S(1)} %copy.17, f32[1024,256]{0,1:T(8,128)S(1)} %fusion.269, f32[256]{0:T(256)S(1)} %broadcast_in_dim.78, f32[256]{0:T(256)S(1)} %broadcast_in_dim.76, ...), kind=kOutput, calls=%fused_computation.104 | convolution fusion | flops 2518622208 | bytes 7015424 | tf_op jit(solution)/shard_map/dot_general | solution.py:94
  299.3 3.9 %convolution_multiply_fusion.1 = f32[1024,256]{0,1:T(8,128)S(1)} fusion(f32[1024,800]{1,0:T(8,128)S(1)} %copy-done.7, f32[800,256]{1,0:T(8,128)S(1)} %convolution_subtract_fusion.1, f32[1024,256]{0,1:T(8,128)S(1)} %copy.17, f32[1024,256]{0,1:T(8,128)S(1)} %fusion.269, f32[256]{0:T(256)S(1)} %broadcast_in_dim.78, f32[256]{0:T(256)S(1)} %broadcast_in_dim.76, ...), kind=kOutput, calls=%fused_computation.90 | convolution fusion | flops 2518417408 | bytes 7244800 | tf_op jit(solution)/shard_map/dot_general | solution.py:88
  303.3 6.2 %multiply_reduce_fusion.1 = (f32[256]{0:T(256)S(1)}, f32[256]{0:T(256)S(1)}, f32[800,256]{1,0:T(8,128)S(1)}) fusion(f32[800,256]{1,0:T(8,128)S(1)} %convolution_subtract_fusion.1, f32[1024,800]{1,0:T(8,128)S(1)} %copy-done.7, f32[1024,256]{0,1:T(8,128)S(1)} %convolution_multiply_fusion.1), kind=kOutput, calls=%fused_computation.386 | convolution fusion | flops 2517605888 | bytes 5965824 | tf_op jit(solution)/shard_map/dot_general | solution.py:94
  309.7 4.0 %convolution_multiply_fusion = f32[1024,256]{0,1:T(8,128)S(1)} fusion(f32[1024,800]{1,0:T(8,128)S(1)} %copy-done.7, f32[800,256]{1,0:T(8,128)S(1)} %convolution_subtract_fusion.1, f32[800,256]{1,0:T(8,128)S(1)} %get-tuple-element.69, f32[256]{0:T(256)S(1)} %add_divide_fusion.1, f32[256]{0:T(256)S(1)} %add_divide_fusion.2, f32[1024,256]{0,1:T(8,128)S(1)} %copy.17, ...), kind=kOutput, calls=%fused_computation.89 | convolution fusion | flops 2519236608 | bytes 8066048 | tf_op jit(solution)/shard_map/dot_general | solution.py:88
  313.7 6.1 %fusion.12 = f32[256]{0:T(256)S(1)} fusion(f32[1024,800]{1,0:T(8,128)S(1)} %copy-done.7, f32[1024,256]{0,1:T(8,128)S(1)} %convolution_multiply_fusion, f32[800,256]{1,0:T(8,128)S(1)} %convolution_subtract_fusion.1, f32[256]{0:T(256)S(1)} %add_divide_fusion.1, f32[800,256]{1,0:T(8,128)S(1)} %get-tuple-element.69, f32[256]{0:T(256)S(1)} %add_divide_fusion.2), kind=kOutput, calls=%fused_computation.147 | convolution fusion | flops 2518015744 | bytes 5966848 | tf_op jit(solution)/shard_map/dot_general | solution.py:94
  325.4 4.4 %collective-permute-done.13 = f32[800,4,16]{0,2,1:T(8,128)S(1)} collective-permute-done((f32[800,4,16]{0,2,1:T(8,128)S(1)}, f32[800,4,16]{0,2,1:T(8,128)S(1)}, u32[]{:S(2)}, u32[]{:S(2)}) %collective-permute-start.13) | collective-permute-done | bytes 204832 | tf_op jit(solution)/shard_map/ppermute | solution.py:28
  329.8 6.0 %fusion.39 = f32[800,16,16]{0,2,1:T(8,128)S(1)} fusion(f32[800,16,16]{0,2,1:T(8,128)S(1)} %bitcast.134, f32[800,4,16]{0,2,1:T(8,128)S(1)} %collective-permute-done.13, f32[800,4,16]{0,2,1:T(8,128)S(1)} %collective-permute-done.12, f32[]{:T(128)} %bitcast.28, f32[]{:T(128)} %bitcast.27, f32[]{:T(128)} %bitcast.26, f32[]{:T(128)} %bitcast.25, f32[]{:T(128)} %bitcast.24, ...), kind=kLoop, calls=%fused_computation.193 | loop fusion | flops 5120000 | bytes 2048036 | tf_op jit(solution)/shard_map/add | solution.py:114
  338.4 3.7 %collective-permute-start.15 = (f32[800,16,4]{0,2,1:T(4,128)S(1)}, f32[800,16,4]{0,2,1:T(4,128)S(1)}, u32[]{:S(2)}, u32[]{:S(2)}) collective-permute-start(f32[800,16,4]{0,2,1:T(4,128)S(1)} %get-tuple-element.34), channel_id=1, source_target_pairs={{1,0},{2,1},{3,2},{4,3},{5,4},{6,5},{7,6},{9,8},{10,9},{11,10},{12... | collective-permute-start | bytes 614408 | tf_op jit(solution)/shard_map/ppermute | solution.py:28
  342.1 4.1 %collective-permute-done.14 = f32[800,16,4]{0,2,1:T(4,128)S(1)} collective-permute-done((f32[800,16,4]{0,2,1:T(4,128)S(1)}, f32[800,16,4]{0,2,1:T(4,128)S(1)}, u32[]{:S(2)}, u32[]{:S(2)}) %collective-permute-start.14) | collective-permute-done | bytes 204832 | tf_op jit(solution)/shard_map/ppermute | solution.py:27
  348.0 6.9 %fusion.119 = f32[800,16,16]{0,2,1:T(8,128)S(1)} fusion(f32[800,16,16]{0,2,1:T(8,128)S(1)} %fusion.39, f32[800,16,4]{0,2,1:T(4,128)S(1)} %collective-permute-done.15, f32[800,16,4]{0,2,1:T(4,128)S(1)} %collective-permute-done.14, f32[]{:T(128)} %bitcast.28, f32[]{:T(128)} %bitcast.27, f32[]{:T(128)} %bitcast.26, f32[]{:T(128)} %bitcast.25, f32[]{:T(128)} %bitcast.24, ...), kind=kLoop, calls=%fused_computation.273 | loop fusion | flops 5120000 | bytes 2048036 | tf_op jit(solution)/shard_map/add | solution.py:124
  (125 shorter events, 86.5 us)
Async XLA Ops:
  30.9 11.4 %copy-start.13 = (s32[1024]{0:T(1024)S(1)}, s32[1024]{0:T(1024)}, u32[]{:S(2)}) copy-start(s32[1024]{0:T(1024)} %param.7) | copy-start | bytes 12292
  30.9 11.4 %copy-start.12 = (s32[1024,2]{0,1:T(2,128)S(1)}, s32[1024,2]{0,1:T(2,128)}, u32[]{:S(2)}) copy-start(s32[1024,2]{0,1:T(2,128)} %param.6) | copy-start | bytes 24580
  30.9 11.4 %copy-start.11 = (s32[2,16,16]{2,1,0:T(8,128)S(1)}, s32[2,16,16]{2,1,0:T(8,128)}, u32[]{:S(2)}) copy-start(s32[2,16,16]{2,1,0:T(8,128)} %param.5) | copy-start | bytes 6148
  35.3 21.6 %all-to-all-start = ((bf16[32,32,256]{2,0,1:T(8,128)(2,1)}), bf16[32,32,256]{2,0,1:T(8,128)(2,1)S(1)}, u32[]{:S(2)}, u32[]{:S(2)}) async-start(bf16[32,32,256]{2,0,1:T(8,128)(2,1)} %copy.16), calls=%async_computation | async-start | bytes 1048576 | tf_op jit(solution)/shard_map/all_to_all | solution.py:171
  43.8 1.8 copy-start
  57.3 8.2 %copy-start.1 = (f32[1024,800]{1,0:T(8,128)S(1)}, f32[1024,800]{1,0:T(8,128)}, u32[]{:S(2)}) copy-start(f32[1024,800]{1,0:T(8,128)} %copy-done) | copy-start | bytes 9830404
  93.2 34.7 %copy-start.2 = (f32[1024,800]{1,0:T(8,128)S(1)}, f32[1024,800]{1,0:T(8,128)}, u32[]{:S(2)}) copy-start(f32[1024,800]{1,0:T(8,128)} %copy-done) | copy-start | bytes 9830404
  93.2 5.9 %collective-permute-start = (f32[800,4,16]{0,2,1:T(8,128)S(1)}, f32[800,4,16]{0,2,1:T(8,128)S(1)}, u32[]{:S(2)}, u32[]{:S(2)}) collective-permute-start(f32[800,4,16]{0,2,1:T(8,128)S(1)} %get-tuple-element.47), channel_id=1, source_target_pairs={{0,8},{8,16},{16,24},{1,9},{9,17},{17,25},{2,10},{10,18},{18,26},{... | collective-permute-start | bytes 614408 | tf_op jit(solution)/shard_map/ppermute | solution.py:27
  96.0 7.3 %collective-permute-start.1 = (f32[800,4,16]{0,2,1:T(8,128)S(1)}, f32[800,4,16]{0,2,1:T(8,128)S(1)}, u32[]{:S(2)}, u32[]{:S(2)}) collective-permute-start(f32[800,4,16]{0,2,1:T(8,128)S(1)} %get-tuple-element.48), channel_id=1, source_target_pairs={{8,0},{16,8},{24,16},{9,1},{17,9},{25,17},{10,2},{18,10},{26,18},{... | collective-permute-start | bytes 614408 | tf_op jit(solution)/shard_map/ppermute | solution.py:28
  109.4 9.4 %collective-permute-start.2 = (f32[800,16,4]{0,2,1:T(4,128)S(1)}, f32[800,16,4]{0,2,1:T(4,128)S(1)}, u32[]{:S(2)}, u32[]{:S(2)}) collective-permute-start(f32[800,16,4]{0,2,1:T(4,128)S(1)} %get-tuple-element.45), channel_id=1, source_target_pairs={{0,1},{1,2},{2,3},{3,4},{4,5},{5,6},{6,7},{8,9},{9,10},{10,11},{11... | collective-permute-start | bytes 614408 | tf_op jit(solution)/shard_map/ppermute | solution.py:27
  111.6 9.4 %collective-permute-start.3 = (f32[800,16,4]{0,2,1:T(4,128)S(1)}, f32[800,16,4]{0,2,1:T(4,128)S(1)}, u32[]{:S(2)}, u32[]{:S(2)}) collective-permute-start(f32[800,16,4]{0,2,1:T(4,128)S(1)} %get-tuple-element.46), channel_id=1, source_target_pairs={{1,0},{2,1},{3,2},{4,3},{5,4},{6,5},{7,6},{9,8},{10,9},{11,10},{12... | collective-permute-start | bytes 614408 | tf_op jit(solution)/shard_map/ppermute | solution.py:28
  132.8 8.4 %copy-start.3 = (f32[1024,800]{1,0:T(8,128)S(1)}, f32[1024,800]{1,0:T(8,128)}, u32[]{:S(2)}) copy-start(f32[1024,800]{1,0:T(8,128)} %copy-done) | copy-start | bytes 9830404
  162.1 6.1 %copy-start.9 = (f32[800,256]{1,0:T(8,128)S(1)}, f32[800,256]{1,0:T(8,128)}, u32[]{:S(2)}) copy-start(f32[800,256]{1,0:T(8,128)} %copy.27) | copy-start | bytes 2457604
  169.1 34.7 %copy-start.4 = (f32[1024,800]{1,0:T(8,128)S(1)}, f32[1024,800]{1,0:T(8,128)}, u32[]{:S(2)}) copy-start(f32[1024,800]{1,0:T(8,128)} %copy-done) | copy-start | bytes 9830404
  169.2 5.3 %collective-permute-start.4 = (f32[800,4,16]{0,2,1:T(8,128)S(1)}, f32[800,4,16]{0,2,1:T(8,128)S(1)}, u32[]{:S(2)}, u32[]{:S(2)}) collective-permute-start(f32[800,4,16]{0,2,1:T(8,128)S(1)} %get-tuple-element.43), channel_id=1, source_target_pairs={{0,8},{8,16},{16,24},{1,9},{9,17},{17,25},{2,10},{10,18},{18,26},{... | collective-permute-start | bytes 614408 | tf_op jit(solution)/shard_map/ppermute | solution.py:27
  171.5 7.3 %collective-permute-start.5 = (f32[800,4,16]{0,2,1:T(8,128)S(1)}, f32[800,4,16]{0,2,1:T(8,128)S(1)}, u32[]{:S(2)}, u32[]{:S(2)}) collective-permute-start(f32[800,4,16]{0,2,1:T(8,128)S(1)} %get-tuple-element.44), channel_id=1, source_target_pairs={{8,0},{16,8},{24,16},{9,1},{17,9},{25,17},{10,2},{18,10},{26,18},{... | collective-permute-start | bytes 614408 | tf_op jit(solution)/shard_map/ppermute | solution.py:28
  185.0 9.8 %collective-permute-start.6 = (f32[800,16,4]{0,2,1:T(4,128)S(1)}, f32[800,16,4]{0,2,1:T(4,128)S(1)}, u32[]{:S(2)}, u32[]{:S(2)}) collective-permute-start(f32[800,16,4]{0,2,1:T(4,128)S(1)} %get-tuple-element.41), channel_id=1, source_target_pairs={{0,1},{1,2},{2,3},{3,4},{4,5},{5,6},{6,7},{8,9},{9,10},{10,11},{11... | collective-permute-start | bytes 614408 | tf_op jit(solution)/shard_map/ppermute | solution.py:27
  186.9 10.0 %collective-permute-start.7 = (f32[800,16,4]{0,2,1:T(4,128)S(1)}, f32[800,16,4]{0,2,1:T(4,128)S(1)}, u32[]{:S(2)}, u32[]{:S(2)}) collective-permute-start(f32[800,16,4]{0,2,1:T(4,128)S(1)} %get-tuple-element.42), channel_id=1, source_target_pairs={{1,0},{2,1},{3,2},{4,3},{5,4},{6,5},{7,6},{9,8},{10,9},{11,10},{12... | collective-permute-start | bytes 614408 | tf_op jit(solution)/shard_map/ppermute | solution.py:28
  208.7 8.4 %copy-start.5 = (f32[1024,800]{1,0:T(8,128)S(1)}, f32[1024,800]{1,0:T(8,128)}, u32[]{:S(2)}) copy-start(f32[1024,800]{1,0:T(8,128)} %copy-done) | copy-start | bytes 9830404
  238.0 6.1 %copy-start.10 = (f32[800,256]{1,0:T(8,128)S(1)}, f32[800,256]{1,0:T(8,128)}, u32[]{:S(2)}) copy-start(f32[800,256]{1,0:T(8,128)} %copy.34) | copy-start | bytes 2457604
  244.8 34.7 %copy-start.6 = (f32[1024,800]{1,0:T(8,128)S(1)}, f32[1024,800]{1,0:T(8,128)}, u32[]{:S(2)}) copy-start(f32[1024,800]{1,0:T(8,128)} %copy-done) | copy-start | bytes 9830404
  244.8 5.1 %collective-permute-start.8 = (f32[800,4,16]{0,2,1:T(8,128)S(1)}, f32[800,4,16]{0,2,1:T(8,128)S(1)}, u32[]{:S(2)}, u32[]{:S(2)}) collective-permute-start(f32[800,4,16]{0,2,1:T(8,128)S(1)} %get-tuple-element.39), channel_id=1, source_target_pairs={{0,8},{8,16},{16,24},{1,9},{9,17},{17,25},{2,10},{10,18},{18,26},{... | collective-permute-start | bytes 614408 | tf_op jit(solution)/shard_map/ppermute | solution.py:27
  247.0 7.3 %collective-permute-start.9 = (f32[800,4,16]{0,2,1:T(8,128)S(1)}, f32[800,4,16]{0,2,1:T(8,128)S(1)}, u32[]{:S(2)}, u32[]{:S(2)}) collective-permute-start(f32[800,4,16]{0,2,1:T(8,128)S(1)} %get-tuple-element.40), channel_id=1, source_target_pairs={{8,0},{16,8},{24,16},{9,1},{17,9},{25,17},{10,2},{18,10},{26,18},{... | collective-permute-start | bytes 614408 | tf_op jit(solution)/shard_map/ppermute | solution.py:28
  260.5 9.9 %collective-permute-start.10 = (f32[800,16,4]{0,2,1:T(4,128)S(1)}, f32[800,16,4]{0,2,1:T(4,128)S(1)}, u32[]{:S(2)}, u32[]{:S(2)}) collective-permute-start(f32[800,16,4]{0,2,1:T(4,128)S(1)} %get-tuple-element.37), channel_id=1, source_target_pairs={{0,1},{1,2},{2,3},{3,4},{4,5},{5,6},{6,7},{8,9},{9,10},{10,11},{11... | collective-permute-start | bytes 614408 | tf_op jit(solution)/shard_map/ppermute | solution.py:27
  262.6 10.0 %collective-permute-start.11 = (f32[800,16,4]{0,2,1:T(4,128)S(1)}, f32[800,16,4]{0,2,1:T(4,128)S(1)}, u32[]{:S(2)}, u32[]{:S(2)}) collective-permute-start(f32[800,16,4]{0,2,1:T(4,128)S(1)} %get-tuple-element.38), channel_id=1, source_target_pairs={{1,0},{2,1},{3,2},{4,3},{5,4},{6,5},{7,6},{9,8},{10,9},{11,10},{12... | collective-permute-start | bytes 614408 | tf_op jit(solution)/shard_map/ppermute | solution.py:28
  284.4 8.4 %copy-start.7 = (f32[1024,800]{1,0:T(8,128)S(1)}, f32[1024,800]{1,0:T(8,128)}, u32[]{:S(2)}) copy-start(f32[1024,800]{1,0:T(8,128)} %copy-done) | copy-start | bytes 9830404
  313.7 6.1 %copy-start.8 = (f32[800,256]{1,0:T(8,128)S(1)}, f32[800,256]{1,0:T(8,128)}, u32[]{:S(2)}) copy-start(f32[800,256]{1,0:T(8,128)} %copy.41) | copy-start | bytes 2457604
  320.5 4.9 %collective-permute-start.12 = (f32[800,4,16]{0,2,1:T(8,128)S(1)}, f32[800,4,16]{0,2,1:T(8,128)S(1)}, u32[]{:S(2)}, u32[]{:S(2)}) collective-permute-start(f32[800,4,16]{0,2,1:T(8,128)S(1)} %get-tuple-element.35), channel_id=1, source_target_pairs={{0,8},{8,16},{16,24},{1,9},{9,17},{17,25},{2,10},{10,18},{18,26},{... | collective-permute-start | bytes 614408 | tf_op jit(solution)/shard_map/ppermute | solution.py:27
  322.5 7.3 %collective-permute-start.13 = (f32[800,4,16]{0,2,1:T(8,128)S(1)}, f32[800,4,16]{0,2,1:T(8,128)S(1)}, u32[]{:S(2)}, u32[]{:S(2)}) collective-permute-start(f32[800,4,16]{0,2,1:T(8,128)S(1)} %get-tuple-element.36), channel_id=1, source_target_pairs={{8,0},{16,8},{24,16},{9,1},{17,9},{25,17},{10,2},{18,10},{26,18},{... | collective-permute-start | bytes 614408 | tf_op jit(solution)/shard_map/ppermute | solution.py:28
  335.9 10.3 %collective-permute-start.14 = (f32[800,16,4]{0,2,1:T(4,128)S(1)}, f32[800,16,4]{0,2,1:T(4,128)S(1)}, u32[]{:S(2)}, u32[]{:S(2)}) collective-permute-start(f32[800,16,4]{0,2,1:T(4,128)S(1)} %get-tuple-element.33), channel_id=1, source_target_pairs={{0,1},{1,2},{2,3},{3,4},{4,5},{5,6},{6,7},{8,9},{9,10},{10,11},{11... | collective-permute-start | bytes 614408 | tf_op jit(solution)/shard_map/ppermute | solution.py:27
  338.4 9.6 %collective-permute-start.15 = (f32[800,16,4]{0,2,1:T(4,128)S(1)}, f32[800,16,4]{0,2,1:T(4,128)S(1)}, u32[]{:S(2)}, u32[]{:S(2)}) collective-permute-start(f32[800,16,4]{0,2,1:T(4,128)S(1)} %get-tuple-element.34), channel_id=1, source_target_pairs={{1,0},{2,1},{3,2},{4,3},{5,4},{6,5},{7,6},{9,8},{10,9},{11,10},{12... | collective-permute-start | bytes 614408 | tf_op jit(solution)/shard_map/ppermute | solution.py:28
where the time goes:
time: 362 us; the launch traced here: 357 us
  matrix products  167 us (46%)
  other arithmetic  59.5 us (16%)
  waiting for transfers between devices  49.4 us (14%)
  starting transfers between devices  49.2 us (14%)
  local copies, waits for them, and re-layouts  31.1 us (9%)
    dot_general x16, matrix products, apply_transpose(): lax.dot_general(matrix, pair_values, (((0,), (0,)), ((), ())), precision=...  109 us
    dot_general x12, matrix products, apply_design(): jnp.dot(matrix, field_in, precision=lax.Precision.HIGHEST, preferred_elem...  46.6 us
    add x4, other arithmetic, cols_pass(): result_sum + tap_values[tap_index] * padded[:, :, tap_index:tap_index + c...  27.5 us
    ppermute x8, waiting for transfers between devices, padded_2(): after = lax.ppermute(first, axis, down)  25.5 us
    ppermute x8, starting transfers between devices, padded_2(): after = lax.ppermute(first, axis, down)  25.2 us
    add x4, other arithmetic, rows_pass(): along_rows + tap_values[tap_index] * padded[:, tap_index:tap_index + rows...  24.2 us
    ppermute x8, starting transfers between devices, padded_2(): before = lax.ppermute(last, axis, up)  17.7 us
    ppermute x8, waiting for transfers between devices, padded_2(): before = lax.ppermute(last, axis, up)  16.3 us
  transfers between devices with their start and end apart: 17, of which 16 were waited for; matrix products, arithmetic and copies ran while one was open for 2% of the time, Pallas kernels for 0%

commit v1 on v0

v1 whole, which is shorter than its diff:
```python
import functools
import math

import jax
import jax.numpy as jnp
import numpy as np
from jax import lax
from jax.experimental import pallas as pl
from jax.experimental.pallas import tpu as pltpu
from jax.sharding import PartitionSpec as P

NEPOCH = 400
ASC = 576
RADIUS = 4
ROUNDS = 4
CG_STEPS = 2


HUBER_EDGE = 0.5
TIKHONOV = 1.0
EPSILON = 1e-06


UP_COEF = (0.8, 0.75)
EAST_COEF = (-0.6, 0.66)
MESH = pl.DeviceIdType.MESH
WHOLE = pl.BlockSpec(memory_space=pltpu.VMEM)


def mm(left, right):
    return jnp.dot(left, right, preferred_element_type=jnp.float32)


def mm_nt(left, right):
    return lax.dot_general(
        left, right, (((1,), (1,)), ((), ())), preferred_element_type=jnp.float32
    )


def mm_tn(left, right):
    return lax.dot_general(
        left, right, (((0,), (0,)), ((), ())), preferred_element_type=jnp.float32
    )


def halves(value):
    high = value.astype(jnp.bfloat16)
    return high, (value - high.astype(jnp.float32)).astype(jnp.bfloat16)


def spectral_tables(side):
    cells = side * side
    index = np.arange(cells)
    row, col = index // side, index % side
    phase = (row[:, None] * row[None, :] + col[:, None] * col[None, :]) % side
    angle = phase * (2.0 * math.pi / side)

    def split(value):
        high = value.astype(np.float32).astype(jnp.bfloat16)
        return high, (value - high.astype(np.float64)).astype(jnp.bfloat16)

    near_row = (row[:, None] - row[None, :] + 1) % side <= 2
    near_col = (col[:, None] - col[None, :] + 1) % side <= 2
    box = (near_row & near_col).astype(np.float32).astype(jnp.bfloat16)
    turn = np.concatenate([np.cos(angle), -np.sin(angle)], axis=0)
    return [jnp.asarray(t) for t in (*split(turn), box)]


def filter_kernel(local, side, x_ref, turn_hi, turn_lo, box_ref, out_ref, cells_ref):
    full_rows = x_ref.shape[1] // local
    full_cols = x_ref.shape[0] * 128
    cells = side * side
    bands = full_rows // side
    group = bands * local
    tiles = full_cols // side
    per_block = 128 // side
    for line in range(side):
        for block in range(full_cols // 128):
            stacked = jnp.concatenate(
                [
                    x_ref[block, pl.ds(band * side + line, local, stride=full_rows), :]
                    for band in range(bands)
                ],
                axis=0,
            )
            flipped = stacked.T
            for inner in range(per_block):
                tile = block * per_block + inner
                cells_ref[
                    line * side : (line + 1) * side, tile * group : (tile + 1) * group
                ] = flipped[inner * side : (inner + 1) * side]
    step = 2
    for first in range(0, tiles, step):
        span = slice(first * group, (first + step) * group)
        high, low = halves(cells_ref[:, span])
        spectrum = mm(turn_hi[...], high) + mm(turn_lo[...], high) + mm(turn_hi[...], low)
        real, imag = spectrum[:cells], spectrum[cells:]
        magnitude = jnp.sqrt(real * real + imag * imag + 1.0)
        high, low = halves(magnitude)
        weight = jnp.sqrt((mm(box_ref[...], high) + mm(box_ref[...], low)) / 9.0)
        mean = jnp.sum(weight, axis=0, keepdims=True) / cells
        scaled = jnp.concatenate([real * weight, imag * weight], axis=0) / (cells * mean)
        high, low = halves(scaled)
        for inner in range(step):
            part = slice(inner * group, (inner + 1) * group)
            restored = (
                mm_tn(high[:, part], turn_hi[...])
                + mm_tn(low[:, part], turn_hi[...])
                + mm_tn(high[:, part], turn_lo[...])
            ).astype(jnp.bfloat16)
            for band in range(bands):
                out_ref[band * tiles + first + inner] = restored[
                    band * local : (band + 1) * local
                ]


def filtered(interferograms, rows_split, side):
    local, full_rows, full_cols = interferograms.shape
    cells = side * side
    tiles = full_cols // side
    tables = spectral_tables(side)
    blocks = interferograms.reshape(local * full_rows, full_cols // 128, 128)
    return pl.pallas_call(
        functools.partial(filter_kernel, local, side),
        out_shape=jax.ShapeDtypeStruct((rows_split * tiles, local, cells), jnp.bfloat16),
        in_specs=[WHOLE] * 4,
        out_specs=WHOLE,
        scratch_shapes=[pltpu.VMEM((cells, tiles * rows_split * local), jnp.float32)],
        compiler_params=pltpu.CompilerParams(vmem_limit_bytes=40 * 1024 * 1024),
        name="filter",
    )(blocks.transpose(1, 0, 2), *tables)


def prepare_kernel(epochs_ref, track_ref, c0_ref, c1_ref, ct0_ref, ct1_ref, perm_ref):
    pairs = track_ref.shape[1]
    ascending = (track_ref[...] == 0).astype(jnp.float32)
    one = jnp.broadcast_to(ascending, (8, pairs)).astype(jnp.bfloat16)
    row_id = lax.broadcasted_iota(jnp.int32, (pairs, pairs), 0)
    col_id = lax.broadcasted_iota(jnp.int32, (pairs, pairs), 1)
    upto = (row_id <= col_id).astype(jnp.float32).astype(jnp.bfloat16)
    count = mm(one, upto)[0:1].astype(jnp.int32)
    place = lax.broadcasted_iota(jnp.int32, (1, pairs), 1)
    position = jnp.where(track_ref[...] == 0, count - 1, ASC + place - count)
    perm = (row_id == position).astype(jnp.float32).astype(jnp.bfloat16)
    perm_ref[...] = perm
    epoch_id = lax.broadcasted_iota(jnp.int32, (NEPOCH, pairs), 0)
    change = (epoch_id == epochs_ref[1:2, :]).astype(jnp.float32) - (
        epoch_id == epochs_ref[0:1, :]
    ).astype(jnp.float32)
    change = change.astype(jnp.bfloat16)
    c0_ref[...] = mm_nt(perm[:ASC], change).astype(jnp.bfloat16)
    c1_ref[...] = mm_nt(perm[ASC:], change).astype(jnp.bfloat16)
    ct0_ref[...] = mm_nt(change, perm[:ASC]).astype(jnp.bfloat16)
    ct1_ref[...] = mm_nt(change, perm[ASC:]).astype(jnp.bfloat16)


def prepare(epochs, track):
    pairs = track.shape[0]
    rest = pairs - ASC
    shapes = ((ASC, NEPOCH), (rest, NEPOCH), (NEPOCH, ASC), (NEPOCH, rest), (pairs, pairs))
    return pl.pallas_call(
        prepare_kernel,
        out_shape=[jax.ShapeDtypeStruct(s, jnp.bfloat16) for s in shapes],
        in_specs=[WHOLE] * 2,
        out_specs=[WHOLE] * 5,
        cost_estimate=pl.CostEstimate(
            flops=6 * pairs * pairs * NEPOCH, bytes_accessed=8 * pairs * pairs, transcendentals=0
        ),
        name="prepare",
    )(epochs.T, track[None, :])


def smoothing_tables(side):
    cells = side * side
    offsets = jnp.arange(-RADIUS, RADIUS + 1).astype(jnp.float32)
    total = jnp.sum(jnp.exp(-offsets * offsets / 8.0))

    def tap(distance):
        near = jnp.abs(distance) <= RADIUS
        value = jnp.exp(-(distance * distance).astype(jnp.float32) / 8.0) / total
        return jnp.where(near, value, 0.0)

    cell = jnp.arange(cells, dtype=jnp.int32)
    row, col = cell // side, cell % side
    strip = jnp.arange(2 * side * RADIUS, dtype=jnp.int32)
    half, inner = strip // (side * RADIUS), strip % (side * RADIUS)
    tables, picks = [], []
    for mine, other, s_mine, s_other in (
        (row, col, inner // side, inner % side),
        (col, row, inner % RADIUS, inner // RADIUS),
    ):
        same = other[:, None] == other[None, :]
        tables.append(jnp.where(same, tap(mine[:, None] - mine[None, :]), 0.0))
        lines = s_other[:, None] == other[None, :]
        for shift in (-RADIUS, side):
            value = jnp.where(lines, tap(s_mine[:, None] + shift - mine[None, :]), 0.0)
            for part in (0, 1):
                tables.append(jnp.where((half == part)[:, None], value, 0.0))
        for first in (0, side - RADIUS):
            hit = (other[:, None] == s_other[None, :]) & (
                mine[:, None] == s_mine[None, :] + first
            )
            for part in (0, 1):
                picks.append((hit & (half == part)[None, :]).astype(jnp.bfloat16))
    own = jnp.stack([tables[0], tables[5]])
    strips = jnp.stack(tables[1:5] + tables[6:10])

    def split(value):
        high = lax.reduce_precision(value, 8, 7)
        return high.astype(jnp.bfloat16), (value - high).astype(jnp.bfloat16)

    return split(own) + split(strips) + (jnp.stack(picks),)


def invert_kernel(
    obs_ref, mask_ref, c0_ref, c1_ref, ct0_ref, ct1_ref, perm_ref,
    own_hi, own_lo, strip_hi, strip_lo, pick_ref,
    out_ref, meas_ref, weight_ref, send_buf, recv_buf, send_sem, recv_sem,
):
    design = (c0_ref, c1_ref)
    transposed = (ct0_ref, ct1_ref)
    spans = (slice(0, ASC), slice(ASC, obs_ref.shape[0]))
    me = {name: lax.axis_index(name) for name in ("pair", "tile")}
    size = {name: lax.axis_size(name) for name in ("pair", "tile")}
    axes = ("pair", "tile")

    def there(axis, step):
        return {"pair": me["pair"], "tile": me["tile"], axis: me[axis] + step}

    def target(axis, step):
        where = there(axis, step)
        return (where["pair"], where["tile"])

    def has(axis, step):
        return me[axis] > 0 if step < 0 else me[axis] < size[axis] - 1

    recv_buf[...] = jnp.zeros_like(recv_buf)
    barrier = pltpu.get_barrier_semaphore()
    for axis in axes:
        for step in (-1, 1):

            @pl.when(has(axis, step))
            def _():
                pl.semaphore_signal(
                    barrier, inc=1, device_id=target(axis, step), device_id_type=MESH
                )

    meas_ref[...] = mm(perm_ref[...], obs_ref[...])
    out_ref[...] = jnp.zeros_like(out_ref)

    peers = sum(
        jnp.where(has(axis, step), 1, 0) for axis in axes for step in (-1, 1)
    )
    pl.semaphore_wait(barrier, peers)

    def forward(field, track, passes):
        mixed = UP_COEF[track] * field[:NEPOCH] + EAST_COEF[track] * field[NEPOCH:]
        high, low = halves(mixed)
        result = mm(design[track][...], high)
        if passes > 1:
            result = result + mm(design[track][...], low)
        return result

    def backward(parts):
        sums = []
        for track in (0, 1):
            high, low = halves(parts[track])
            sums.append(mm(transposed[track][...], high) + mm(transposed[track][...], low))
        return jnp.concatenate(
            [
                UP_COEF[0] * sums[0] + UP_COEF[1] * sums[1],
                EAST_COEF[0] * sums[0] + EAST_COEF[1] * sums[1],
            ],
            axis=0,
        )

    def total(value):
        return jnp.sum(value, axis=0, keepdims=True)

    def exchange(turn, which, field_hi):
        axis = axes[which]
        copies = []
        for side, step in ((0, -1), (1, 1)):
            slot = 2 * which + side
            edge = mm(field_hi[:NEPOCH], pick_ref[2 * slot]) + mm(
                field_hi[NEPOCH:], pick_ref[2 * slot + 1]
            )
            send_buf[turn, slot] = edge.astype(jnp.bfloat16)
            landing = 2 * which + 1 - side
            copy = pltpu.make_async_remote_copy(
                src_ref=send_buf.at[turn, slot],
                dst_ref=recv_buf.at[turn, landing],
                send_sem=send_sem.at[turn, slot],
                recv_sem=recv_sem.at[turn, landing],
                device_id=target(axis, step),
                device_id_type=MESH,
            )

            @pl.when(has(axis, step))
            def _():
                copy.start()

            copies.append((copy, axis, step, slot))
        return copies

    def smooth_own(which, high, low):
        return mm(high, own_hi[which]) + mm(high, own_lo[which]) + mm(low, own_hi[which])

    def finish(turn, which, copies):
        for copy, axis, step, slot in copies:
            incoming = pltpu.make_async_remote_copy(
                src_ref=send_buf.at[turn, slot],
                dst_ref=recv_buf.at[turn, slot],
                send_sem=send_sem.at[turn, slot],
                recv_sem=recv_sem.at[turn, slot],
                device_id=target(axis, step),
                device_id_type=MESH,
            )

            @pl.when(has(axis, step))
            def _():
                copy.wait_send()
                incoming.wait_recv()

        parts = []
        for part in (0, 1):
            value = 0.0
            for side in (0, 1):
                slot = 2 * which + side
                index = 2 * slot + part
                edge = recv_buf[turn, slot]
                value = value + mm(edge, strip_hi[index]) + mm(edge, strip_lo[index])
            parts.append(value)
        return jnp.concatenate(parts, axis=0)

    def one_round(turn, carry):
        solution = out_ref[...]
        pulls = []
        for track in (0, 1):
            misfit = meas_ref[spans[track]] - forward(solution, track, 2)
            weight = mask_ref[track : track + 1] * HUBER_EDGE / jnp.maximum(
                jnp.abs(misfit), HUBER_EDGE
            )
            weight_ref[spans[track]] = weight
            pulls.append(weight * misfit)
        residual = backward(pulls) - TIKHONOV * solution
        norm = total(residual * residual)
        pulls, curve = [], TIKHONOV * norm
        for track in (0, 1):
            image = forward(residual, track, 2)
            pull = weight_ref[spans[track]] * image
            curve = curve + total(pull * image)
            pulls.append(pull)
        step_len = norm / (curve + EPSILON)
        solution = solution + step_len * residual
        after = residual - step_len * (backward(pulls) + TIKHONOV * residual)
        norm_next = total(after * after)
        direction = after + norm_next / (norm + EPSILON) * residual
        curve = TIKHONOV * total(direction * direction)
        for track in (0, 1):
            image = forward(direction, track, 1)
            curve = curve + total(weight_ref[spans[track]] * image * image)
        solution = solution + norm_next / (curve + EPSILON) * direction
        for which in (0, 1):
            high, low = halves(solution)
            copies = exchange(turn, which, high)
            solution = smooth_own(which, high, low)
            solution = solution + finish(turn, which, copies)
        out_ref[...] = solution
        return carry

    lax.fori_loop(0, ROUNDS, one_round, 0)


def invert(observed, mask_cells, epochs, track, side):
    pairs, cells = observed.shape
    strip = 2 * side * RADIUS
    tables = smoothing_tables(side)
    return pl.pallas_call(
        invert_kernel,
        out_shape=jax.ShapeDtypeStruct((2 * NEPOCH, cells), jnp.float32),
        in_specs=[WHOLE] * 12,
        out_specs=WHOLE,
        scratch_shapes=[
            pltpu.VMEM((pairs, cells), jnp.float32),
            pltpu.VMEM((pairs, cells), jnp.float32),
            pltpu.VMEM((ROUNDS, 4, NEPOCH, strip), jnp.bfloat16),
            pltpu.VMEM((ROUNDS, 4, NEPOCH, strip), jnp.bfloat16),
            pltpu.SemaphoreType.DMA((ROUNDS, 4)),
            pltpu.SemaphoreType.DMA((ROUNDS, 4)),
        ],
        compiler_params=pltpu.CompilerParams(
            collective_id=0, has_side_effects=True, vmem_limit_bytes=60 * 1024 * 1024
        ),
        name="invert",
    )(observed, mask_cells, *prepare(epochs, track), *tables)


def per_device(interferograms, coherence, epochs, track):
    rows_split = lax.axis_size("pair")
    local_pairs, full_rows, full_cols = interferograms.shape
    patch_len = full_rows // rows_split
    cell_count = patch_len * patch_len
    cleaned = filtered(interferograms, rows_split, patch_len)
    received = lax.all_to_all(
        cleaned,
        ("pair", "tile"),
        split_axis=0,
        concat_axis=0,
        tiled=True,
    )
    observed = received.reshape(-1, cell_count)
    mask_cells = coherence.reshape(2, cell_count).astype(jnp.float32)

    solution = invert(observed, mask_cells, epochs, track, patch_len)
    return solution.reshape(2, NEPOCH, patch_len, patch_len)


def solution(mesh):
    placed = (P(("pair", "tile"), None, None), P(None, "pair", "tile"), P(), P())
    return jax.shard_map(
        per_device,
        mesh=mesh,
        in_specs=placed,
        out_specs=P(None, None, "pair", "tile"),
        check_vma=False,
    )
```

time: 362 us -> 103 us (0.28); the launches traced: 357 us -> 103 us
  matrix products: 167 us -> 0 us
  Pallas kernels: 0 us -> 74.6 us
  waiting for transfers between devices: 49.4 us -> 0.01 us
  other arithmetic: 59.5 us -> 12.1 us
  starting transfers between devices: 49.2 us -> 6.32 us
  local copies, waits for them, and re-layouts: 31.1 us -> 9.35 us
    dot_general x32 -> x0, matrix products: 167 us -> none  [the longest x16 109 us: apply_transpose(): lax.dot_general(matrix, pair_values, (((0,), (0,)), ((), ())), precision=...]
    pallas_call x0 -> x3, Pallas kernels: none -> 74.6 us  [the longest x1 63.4 us: invert(): pl.pallas_call(invert_kernel, out_shape=jax.ShapeDtypeStruct((2 * NEPOCH,...]
    add x13 -> x4, other arithmetic: 54.1 us -> 0.03 us  [the longest x2 0.01 us: smoothing_tables(): s_mine[None, :] + first]
    ppermute x16 -> x0, starting transfers between devices: 42.9 us -> none  [the longest x8 25.2 us: padded_2(): after = lax.ppermute(first, axis, down)]
    ppermute x16 -> x0, waiting for transfers between devices: 41.8 us -> none  [the longest x8 25.5 us: padded_2(): after = lax.ppermute(first, axis, down)]
    transpose x1 -> x0, local copies, waits for them, and re-layouts: 8.98 us -> none  [per_device(): blocks.transpose(0, 1, 3, 2, 4).reshape(local_pairs, tile_count, cell_count)]
    another operation x3 -> x0, local copies, waits for them, and re-layouts: 8.65 us -> none  [the longest x1 6.27 us: per_device(): blocks.reshape(-1, cell_count)]
    all_to_all x1, waiting for transfers between devices: 7.57 us -> 0.01 us  [per_device(): lax.all_to_all(cleaned, ('pair', 'tile'), split_axis=0, concat_axis=0, ti...]
  transfers between devices with their start and end apart: 17 -> 1, of which waited for: 16 -> 0; matrix products, arithmetic and copies ran while one was open for 2% -> 12% of each run, Pallas kernels for 0% -> 5%
where the time goes in v1:
time: 103 us
  Pallas kernels  74.6 us (72%)
  other arithmetic  12.1 us (12%)
  local copies, waits for them, and re-layouts  9.35 us (9%)
  starting transfers between devices  6.32 us (6%)
    pallas_call x1, Pallas kernels, invert(): pl.pallas_call(invert_kernel, out_shape=jax.ShapeDtypeStruct((2 * NEPOCH,...  63.4 us
    unnamed x14, other arithmetic  6.54 us
    all_to_all x1, starting transfers between devices, per_device(): lax.all_to_all(cleaned, ('pair', 'tile'), split_axis=0, concat_axis=0, ti...  6.32 us
    pallas_call x1, Pallas kernels, filtered(): pl.pallas_call(functools.partial(filter_kernel, local, side), out_shape=j...  5.99 us
    pallas_call x1, Pallas kernels, prepare(): pl.pallas_call(prepare_kernel, out_shape=[jax.ShapeDtypeStruct(s, jnp.bfl...  5.27 us
    unnamed x12, local copies, waits for them, and re-layouts  4.85 us
    reshape x2, local copies, waits for them, and re-layouts, per_device(): return solution.reshape(2, NEPOCH, patch_len, patch_len)  2.38 us
  transfers between devices with their start and end apart: 1, of which 0 were waited for; matrix products, arithmetic and copies ran while one was open for 12% of the time, Pallas kernels for 5%

profile of v1, /device:TPU:9, one launch (start us, length us, event | category | flops | bytes accessed | tf_op | source)
XLA Modules:
  0.0 102.6 jit_solution(499039501061884481)
XLA Ops:
  0.0 0.0 copy-start
  0.0 1.2 %copy-done = f32[32,64,128]{2,1,0:T(8,128)S(1)} copy-done((f32[32,64,128]{2,1,0:T(8,128)S(1)}, f32[32,64,128]{2,1,0:T(8,128)}, u32[]{:S(2)}) %copy-start) | copy-done | bytes 1048600
  1.2 0.0 copy-start.1
  1.2 0.9 copy-done.1
  2.2 0.0 copy-start.2
  2.2 0.9 copy-done.2
  3.1 0.0 copy-start.3
  3.1 0.9 copy-done.3
  4.0 6.0 %filter.1 = bf16[32,32,256]{2,1,0:T(8,128)(2,1)} custom-call(f32[1,2048,128]{2,1,0:T(8,128)S(1)} %bitcast.6, bf16[512,256]{1,0:T(8,128)(2,1)S(1)} %copy-done.2, bf16[512,256]{1,0:T(8,128)(2,1)S(1)} %copy-done.1, bf16[256,256]{1,0:T(8,128)(2,1)S(1)} %copy-done.3), custom_call_target="tpu_custom_call" | custom-call | tf_op jit(solution)/shard_map/filter/pallas_call | solution.py:123
  10.0 0.0 copy-start.5
  10.0 6.3 %all-to-all-start = ((bf16[32,32,256]{2,1,0:T(8,128)(2,1)}), bf16[32,32,256]{2,1,0:T(8,128)(2,1)S(1)}, u32[]{:S(2)}, u32[]{:S(2)}) async-start(bf16[32,32,256]{2,1,0:T(8,128)(2,1)} %filter.1), calls=%async_computation | async-start | bytes 1048576 | tf_op jit(solution)/shard_map/all_to_all | solution.py:405
  16.4 0.6 fusion.49
  17.1 0.1 and_dynamic-update-slice_fusion.7
  17.2 0.2 and_dynamic-update-slice_fusion.6
  17.4 0.2 and_dynamic-update-slice_fusion.5
  17.6 0.2 and_dynamic-update-slice_fusion.4
  17.7 0.2 and_dynamic-update-slice_fusion.3
  17.9 0.2 and_dynamic-update-slice_fusion.2
  18.0 0.2 and_dynamic-update-slice_fusion.1
  18.2 0.2 and_dynamic-update-slice_fusion
  18.4 1.0 fusion.9
  19.3 0.8 select_dynamic-update-slice_fusion.7
  20.1 0.8 select_dynamic-update-slice_fusion.6
  20.9 0.8 select_dynamic-update-slice_fusion.5
  21.7 0.8 select_dynamic-update-slice_fusion.4
  22.5 0.8 select_dynamic-update-slice_fusion.3
  23.3 0.8 select_dynamic-update-slice_fusion.2
  24.1 0.9 fusion.1
  24.9 0.0 copy-done.5
  25.0 0.7 convert_element_type.161.mask_ref
  25.6 0.9 stack.11.pick_ref
  26.6 0.8 select_dynamic-update-slice_fusion.1
  27.3 0.8 select_dynamic-update-slice_fusion
  28.1 5.3 %prepare.1 = (bf16[576,400]{1,0:T(8,128)(2,1)}, bf16[448,400]{1,0:T(8,128)(2,1)}, bf16[400,576]{1,0:T(8,128)(2,1)}, bf16[400,448]{1,0:T(8,128)(2,1)}, bf16[1024,1024]{1,0:T(8,128)(2,1)}) custom-call(s32[2,1024]{1,0:T(2,128)} %bitcast.8, s32[1,1024]{1,0:T(1,128)} %bitcast.9), custom_call_target="tpu_custom_call" | custom-call | flops 2516582400 | bytes 8388608 | tf_op jit(solution)/shard_map/prepare/pallas_call | solution.py:161
  33.4 1.2 %fusion = (bf16[8,128,256]{2,1,0:T(8,128)(2,1)}, bf16[8,128,256]{2,1,0:T(8,128)(2,1)}) fusion(f32[8,128,256]{2,1,0:T(8,128)S(1)} %select_dynamic-update-slice_fusion), kind=kLoop, calls=%fused_computation.2 | loop fusion | flops 1048576 | bytes 2097152 | tf_op jit(solution)/shard_map/convert_element_type | solution.py:210
  34.6 0.0 all-to-all-done
  34.6 0.0 copy-start.4
  34.6 0.8 copy-done.4
  35.4 63.4 %invert.1 = f32[800,256]{1,0:T(8,128)} custom-call(bf16[1024,256]{1,0:T(8,128)(2,1)} %bitcast.7, f32[2,256]{1,0:T(2,128)} %convert_element_type.161.mask_ref, bf16[576,400]{1,0:T(8,128)(2,1)} %get-tuple-element.10.c0_ref, bf16[448,400]{1,0:T(8,128)(2,1)} %get-tuple-element.11.c1_ref, bf16[400,576]{1,0:T(8,128)(2,1)} %get-tuple-element.12.ct0_ref, ...), custom_call_target="tpu_custom_call" | custom-call | tf_op jit(solution)/shard_map/invert/pallas_call | solution.py:379
  98.8 1.4 %copy.9 = f32[800,256]{0,1:T(8,128)S(1)} copy(f32[800,256]{1,0:T(8,128)} %invert.1) | data formatting | bytes 1638400 | tf_op jit(solution)/shard_map/invert/pallas_call | solution.py:379
  100.2 1.2 %reshape.2303 = f32[2,400,16,16]{1,0,3,2:T(2,128)S(1)} reshape(f32[800,256]{0,1:T(8,128)S(1)} %copy.9) | data formatting | bytes 1638400 | tf_op jit(solution)/shard_map/reshape | solution.py:416
  101.4 1.2 %copy.10 = f32[2,400,16,16]{1,3,2,0:T(8,128)} copy(f32[2,400,16,16]{1,0,3,2:T(2,128)S(1)} %reshape.2303) | data formatting | bytes 1638400 | tf_op jit(solution)/shard_map/reshape | solution.py:416
  (12 shorter events, 0.1 us)
Async XLA Ops:
  0.0 1.2 %copy-start = (f32[32,64,128]{2,1,0:T(8,128)S(1)}, f32[32,64,128]{2,1,0:T(8,128)}, u32[]{:S(2)}) copy-start(f32[32,64,128]{2,1,0:T(8,128)} %param.7) | copy-start | bytes 3145732
  1.2 0.9 copy-start.1
  2.2 0.9 copy-start.2
  3.1 0.9 copy-start.3
  10.0 14.9 %copy-start.5 = (s32[2,16,16]{2,1,0:T(8,128)S(1)}, s32[2,16,16]{2,1,0:T(8,128)}, u32[]{:S(2)}) copy-start(s32[2,16,16]{2,1,0:T(8,128)} %param.8) | copy-start | bytes 6148
  10.0 24.5 %all-to-all-start = ((bf16[32,32,256]{2,1,0:T(8,128)(2,1)}), bf16[32,32,256]{2,1,0:T(8,128)(2,1)S(1)}, u32[]{:S(2)}, u32[]{:S(2)}) async-start(bf16[32,32,256]{2,1,0:T(8,128)(2,1)} %filter.1), calls=%async_computation | async-start | bytes 1048576 | tf_op jit(solution)/shard_map/all_to_all | solution.py:405
  34.6 0.8 copy-start.4

commit v2 on v1

--- a/solution.py
+++ b/solution.py
@@ -48,6 +48,11 @@
     return high, (value - high.astype(jnp.float32)).astype(jnp.bfloat16)
 
 
+def split_table(value):
+    high = value.astype(np.float32).astype(jnp.bfloat16)
+    return high, (value - high.astype(np.float64)).astype(jnp.bfloat16)
+
+
 def spectral_tables(side):
     cells = side * side
     index = np.arange(cells)
@@ -55,18 +60,26 @@
     phase = (row[:, None] * row[None, :] + col[:, None] * col[None, :]) % side
     angle = phase * (2.0 * math.pi / side)
 
-    def split(value):
-        high = value.astype(np.float32).astype(jnp.bfloat16)
-        return high, (value - high.astype(np.float64)).astype(jnp.bfloat16)
-
     near_row = (row[:, None] - row[None, :] + 1) % side <= 2
     near_col = (col[:, None] - col[None, :] + 1) % side <= 2
     box = (near_row & near_col).astype(np.float32).astype(jnp.bfloat16)
     turn = np.concatenate([np.cos(angle), -np.sin(angle)], axis=0)
-    return [jnp.asarray(t) for t in (*split(turn), box)]
-
-
-def filter_kernel(local, side, x_ref, turn_hi, turn_lo, box_ref, out_ref, cells_ref):
+    return [jnp.asarray(t) for t in (*split_table(turn), box)]
+
+
+def filter_kernel(
+    local, side, x_hbm, hi_hbm, lo_hbm, box_hbm, out_ref,
+    cells_ref, x_ref, turn_hi, turn_lo, box_ref, sems,
+):
+    fetches = [
+        pltpu.make_async_copy(source, held, sems.at[number])
+        for number, (source, held) in enumerate(
+            ((x_hbm, x_ref), (hi_hbm, turn_hi), (lo_hbm, turn_lo), (box_hbm, box_ref))
+        )
+    ]
+    for fetch in fetches:
+        fetch.start()
+    fetches[0].wait()
     full_rows = x_ref.shape[1] // local
     full_cols = x_ref.shape[0] * 128
     cells = side * side
@@ -89,6 +102,8 @@
                 cells_ref[
                     line * side : (line + 1) * side, tile * group : (tile + 1) * group
                 ] = flipped[inner * side : (inner + 1) * side]
+    for fetch in fetches[1:]:
+        fetch.wait()
     step = 2
     for first in range(0, tiles, step):
         span = slice(first * group, (first + step) * group)
@@ -123,9 +138,16 @@
     return pl.pallas_call(
         functools.partial(filter_kernel, local, side),
         out_shape=jax.ShapeDtypeStruct((rows_split * tiles, local, cells), jnp.bfloat16),
-        in_specs=[WHOLE] * 4,
+        in_specs=[pl.BlockSpec(memory_space=pltpu.HBM)] * 4,
         out_specs=WHOLE,
-        scratch_shapes=[pltpu.VMEM((cells, tiles * rows_split * local), jnp.float32)],
+        scratch_shapes=[
+            pltpu.VMEM((cells, tiles * rows_split * local), jnp.float32),
+            pltpu.VMEM((full_cols // 128, local * full_rows, 128), jnp.float32),
+            pltpu.VMEM((2 * cells, cells), jnp.bfloat16),
+            pltpu.VMEM((2 * cells, cells), jnp.bfloat16),
+            pltpu.VMEM((cells, cells), jnp.bfloat16),
+            pltpu.SemaphoreType.DMA((4,)),
+        ],
         compiler_params=pltpu.CompilerParams(vmem_limit_bytes=40 * 1024 * 1024),
         name="filter",
     )(blocks.transpose(1, 0, 2), *tables)
@@ -172,44 +194,32 @@
 
 def smoothing_tables(side):
     cells = side * side
-    offsets = jnp.arange(-RADIUS, RADIUS + 1).astype(jnp.float32)
-    total = jnp.sum(jnp.exp(-offsets * offsets / 8.0))
+    offsets = np.arange(-RADIUS, RADIUS + 1)
+    total = np.sum(np.exp(-offsets * offsets / 8.0))
 
     def tap(distance):
-        near = jnp.abs(distance) <= RADIUS
-        value = jnp.exp(-(distance * distance).astype(jnp.float32) / 8.0) / total
-        return jnp.where(near, value, 0.0)
-
-    cell = jnp.arange(cells, dtype=jnp.int32)
+        return np.where(np.abs(distance) <= RADIUS, np.exp(-distance * distance / 8.0) / total, 0.0)
+
+    cell = np.arange(cells)
     row, col = cell // side, cell % side
-    strip = jnp.arange(2 * side * RADIUS, dtype=jnp.int32)
-    half, inner = strip // (side * RADIUS), strip % (side * RADIUS)
-    tables, picks = [], []
+    inner = np.arange(side * RADIUS)
+    own, strips, picks = [], [], []
     for mine, other, s_mine, s_other in (
         (row, col, inner // side, inner % side),
         (col, row, inner % RADIUS, inner // RADIUS),
     ):
         same = other[:, None] == other[None, :]
-        tables.append(jnp.where(same, tap(mine[:, None] - mine[None, :]), 0.0))
+        own.append(np.where(same, tap(mine[:, None] - mine[None, :]), 0.0))
         lines = s_other[:, None] == other[None, :]
         for shift in (-RADIUS, side):
-            value = jnp.where(lines, tap(s_mine[:, None] + shift - mine[None, :]), 0.0)
-            for part in (0, 1):
-                tables.append(jnp.where((half == part)[:, None], value, 0.0))
+            strips.append(np.where(lines, tap(s_mine[:, None] + shift - mine[None, :]), 0.0))
         for first in (0, side - RADIUS):
             hit = (other[:, None] == s_other[None, :]) & (
                 mine[:, None] == s_mine[None, :] + first
             )
-            for part in (0, 1):
-                picks.append((hit & (half == part)[None, :]).astype(jnp.bfloat16))
-    own = jnp.stack([tables[0], tables[5]])
-    strips = jnp.stack(tables[1:5] + tables[6:10])
-
-    def split(value):
-        high = lax.reduce_precision(value, 8, 7)
-        return high.astype(jnp.bfloat16), (value - high).astype(jnp.bfloat16)
-
-    return split(own) + split(strips) + (jnp.stack(picks),)
+            picks.append(hit.astype(np.float32).astype(jnp.bfloat16))
+    tables = (*split_table(np.stack(own)), *split_table(np.stack(strips)), np.stack(picks))
+    return [jnp.asarray(table) for table in tables]
 
 
 def invert_kernel(
@@ -282,10 +292,10 @@
         copies = []
         for side, step in ((0, -1), (1, 1)):
             slot = 2 * which + side
-            edge = mm(field_hi[:NEPOCH], pick_ref[2 * slot]) + mm(
-                field_hi[NEPOCH:], pick_ref[2 * slot + 1]
-            )
-            send_buf[turn, slot] = edge.astype(jnp.bfloat16)
+            edge = mm(field_hi, pick_ref[slot])
+            send_buf[turn, slot] = jnp.concatenate(
+                [edge[:NEPOCH], edge[NEPOCH:]], axis=1
+            ).astype(jnp.bfloat16)
             landing = 2 * which + 1 - side
             copy = pltpu.make_async_remote_copy(
                 src_ref=send_buf.at[turn, slot],
@@ -327,9 +337,9 @@
             value = 0.0
             for side in (0, 1):
                 slot = 2 * which + side
-                index = 2 * slot + part
-                edge = recv_buf[turn, slot]
-                value = value + mm(edge, strip_hi[index]) + mm(edge, strip_lo[index])
+                width = strip_hi.shape[1]
+                edge = recv_buf[turn, slot, :, part * width : (part + 1) * width]
+                value = value + mm(edge, strip_hi[slot]) + mm(edge, strip_lo[slot])
             parts.append(value)
         return jnp.concatenate(parts, axis=0)
 

time: 103 us -> 99.3 us (0.964)
  other arithmetic: 12.1 us -> 0.01 us
  waiting for transfers between devices: 0.01 us -> 9.29 us
    all_to_all x1, waiting for transfers between devices: 0.01 us -> 9.29 us  [per_device(): lax.all_to_all(cleaned, ('pair', 'tile'), split_axis=0, concat_axis=0, ti...]
    unnamed x14 -> x0, other arithmetic: 6.54 us -> none
    convert_element_type x2 -> x0, other arithmetic: 2.03 us -> none  [split(): return (high.astype(jnp.bfloat16), (value - high).astype(jnp.bfloat16))]
    another operation x3 -> x0, other arithmetic: 1.86 us -> none  [the longest x2 1.08 us: smoothing_tables(): return split(own) + split(strips) + (jnp.stack(picks),)]
    pallas_call x1, Pallas kernels: 63.4 us -> 62 us  [invert(): pl.pallas_call(invert_kernel, out_shape=jax.ShapeDtypeStruct((2 * NEPOCH,...]
  transfers between devices with their start and end apart: 1 -> 1, of which waited for: 0 -> 1; matrix products, arithmetic and copies ran while one was open for 12% -> 1% of each run, Pallas kernels for 5% -> 5%
where the time goes in v2:
time: 99.3 us; the launch traced here: 98.6 us
  Pallas kernels  73.6 us (74%)
  local copies, waits for them, and re-layouts  9.3 us (9%)
  waiting for transfers between devices  9.29 us (9%)
  starting transfers between devices  6.33 us (6%)
    pallas_call x1, Pallas kernels, invert(): pl.pallas_call(invert_kernel, out_shape=jax.ShapeDtypeStruct((2 * NEPOCH,...  62 us
    all_to_all x1, waiting for transfers between devices, per_device(): lax.all_to_all(cleaned, ('pair', 'tile'), split_axis=0, concat_axis=0, ti...  9.29 us
    pallas_call x1, Pallas kernels, filtered(): pl.pallas_call(functools.partial(filter_kernel, local, side), out_shape=j...  6.35 us
    all_to_all x1, starting transfers between devices, per_device(): lax.all_to_all(cleaned, ('pair', 'tile'), split_axis=0, concat_axis=0, ti...  6.33 us
    pallas_call x1, Pallas kernels, prepare(): pl.pallas_call(prepare_kernel, out_shape=[jax.ShapeDtypeStruct(s, jnp.bfl...  5.28 us
    unnamed x12, local copies, waits for them, and re-layouts  4.83 us
    reshape x2, local copies, waits for them, and re-layouts, per_device(): return solution.reshape(2, NEPOCH, patch_len, patch_len)  2.38 us
  transfers between devices with their start and end apart: 1, of which 1 were waited for; matrix products, arithmetic and copies ran while one was open for 1% of the time, Pallas kernels for 5%

profile of v2, /device:TPU:9, one launch (start us, length us, event | category | flops | bytes accessed | tf_op | source)
XLA Modules:
  0.0 98.6 jit_solution(9385122492681227696)
XLA Ops:
  0.0 0.0 copy-start
  0.0 1.2 %copy-done = f32[32,64,128]{2,1,0:T(8,128)S(1)} copy-done((f32[32,64,128]{2,1,0:T(8,128)S(1)}, f32[32,64,128]{2,1,0:T(8,128)}, u32[]{:S(2)}) %copy-start) | copy-done | bytes 1048600
  1.2 0.0 copy-start.1
  1.2 0.9 copy-done.1
  2.2 0.0 copy-start.2
  2.2 0.9 copy-done.2
  3.1 0.0 copy-start.3
  3.1 0.9 copy-done.3
  4.0 0.0 copy-start.5
  4.0 6.4 %filter.1 = bf16[32,32,256]{2,1,0:T(8,128)(2,1)} custom-call(f32[1,2048,128]{2,1,0:T(8,128)S(1)} %bitcast.6, bf16[512,256]{1,0:T(8,128)(2,1)S(1)} %copy-done.2, bf16[512,256]{1,0:T(8,128)(2,1)S(1)} %copy-done.1, bf16[256,256]{1,0:T(8,128)(2,1)S(1)} %copy-done.3), custom_call_target="tpu_custom_call" | custom-call | tf_op jit(solution)/shard_map/filter/pallas_call | solution.py:138
  10.4 6.3 %all-to-all-start = ((bf16[32,32,256]{2,1,0:T(8,128)(2,1)}), bf16[32,32,256]{2,1,0:T(8,128)(2,1)S(1)}, u32[]{:S(2)}, u32[]{:S(2)}) async-start(bf16[32,32,256]{2,1,0:T(8,128)(2,1)} %filter.1), calls=%async_computation | async-start | bytes 1048576 | tf_op jit(solution)/shard_map/all_to_all | solution.py:415
  16.7 0.0 copy-done.5
  16.8 0.7 convert_element_type.6.mask_ref
  17.4 5.3 %prepare.1 = (bf16[576,400]{1,0:T(8,128)(2,1)}, bf16[448,400]{1,0:T(8,128)(2,1)}, bf16[400,576]{1,0:T(8,128)(2,1)}, bf16[400,448]{1,0:T(8,128)(2,1)}, bf16[1024,1024]{1,0:T(8,128)(2,1)}) custom-call(s32[2,1024]{1,0:T(2,128)} %bitcast.8, s32[1,1024]{1,0:T(1,128)} %bitcast.9), custom_call_target="tpu_custom_call" | custom-call | flops 2516582400 | bytes 8388608 | tf_op jit(solution)/shard_map/prepare/pallas_call | solution.py:183
  22.7 9.3 %all-to-all-done = bf16[32,32,256]{2,1,0:T(8,128)(2,1)S(1)} async-done(((bf16[32,32,256]{2,1,0:T(8,128)(2,1)}), bf16[32,32,256]{2,1,0:T(8,128)(2,1)S(1)}, u32[]{:S(2)}, u32[]{:S(2)}) %all-to-all-start) | async-done | bytes 524320 | tf_op jit(solution)/shard_map/all_to_all | solution.py:415
  32.0 0.0 copy-start.4
  32.0 0.8 copy-done.4
  32.8 62.0 %invert.1 = f32[800,256]{1,0:T(8,128)} custom-call(bf16[1024,256]{1,0:T(8,128)(2,1)} %bitcast.7, f32[2,256]{1,0:T(2,128)} %convert_element_type.6.mask_ref, bf16[576,400]{1,0:T(8,128)(2,1)} %get-tuple-element.10.c0_ref, bf16[448,400]{1,0:T(8,128)(2,1)} %get-tuple-element.11.c1_ref, bf16[400,576]{1,0:T(8,128)(2,1)} %get-tuple-element.12.ct0_ref, ...), custom_call_target="tpu_custom_call" | custom-call | tf_op jit(solution)/shard_map/invert/pallas_call | solution.py:389
  94.7 1.4 %copy.14 = f32[800,256]{0,1:T(8,128)S(1)} copy(f32[800,256]{1,0:T(8,128)} %invert.1) | data formatting | bytes 1638400 | tf_op jit(solution)/shard_map/invert/pallas_call | solution.py:389
  96.2 1.2 %reshape.9 = f32[2,400,16,16]{1,0,3,2:T(2,128)S(1)} reshape(f32[800,256]{0,1:T(8,128)S(1)} %copy.14) | data formatting | bytes 1638400 | tf_op jit(solution)/shard_map/reshape | solution.py:426
  97.4 1.2 %copy.15 = f32[2,400,16,16]{1,3,2,0:T(8,128)} copy(f32[2,400,16,16]{1,0,3,2:T(2,128)S(1)} %reshape.9) | data formatting | bytes 1638400 | tf_op jit(solution)/shard_map/reshape | solution.py:426
  (1 shorter events, 0.0 us)
Async XLA Ops:
  0.0 1.2 %copy-start = (f32[32,64,128]{2,1,0:T(8,128)S(1)}, f32[32,64,128]{2,1,0:T(8,128)}, u32[]{:S(2)}) copy-start(f32[32,64,128]{2,1,0:T(8,128)} %param.12) | copy-start | bytes 3145732
  1.2 0.9 copy-start.1
  2.2 0.9 copy-start.2
  3.1 0.9 copy-start.3
  4.0 12.7 %copy-start.5 = (s32[2,16,16]{2,1,0:T(8,128)S(1)}, s32[2,16,16]{2,1,0:T(8,128)}, u32[]{:S(2)}) copy-start(s32[2,16,16]{2,1,0:T(8,128)} %param.13) | copy-start | bytes 6148
  10.4 21.6 %all-to-all-start = ((bf16[32,32,256]{2,1,0:T(8,128)(2,1)}), bf16[32,32,256]{2,1,0:T(8,128)(2,1)S(1)}, u32[]{:S(2)}, u32[]{:S(2)}) async-start(bf16[32,32,256]{2,1,0:T(8,128)(2,1)} %filter.1), calls=%async_computation | async-start | bytes 1048576 | tf_op jit(solution)/shard_map/all_to_all | solution.py:415
  32.0 0.8 copy-start.4
